TPU v7x, 256 devices: a whole 4x4x8 slice. The times are simulated.
256 devices in a mesh: gx: 4 (over y), gy: 8 (over x, core), gz: 8 (over z).
Axes of the slice: x: 4, y: 4, z: 8, core: 2. Of those that a mesh axis runs over, the one named last changes fastest.
Arguments:
- data: float32 [128, 256, 1024], P('gx', 'gy', 'gz'), may hold values from -120 to 120
- weights: float32 [8, 1024], P(None, 'gz'), may hold values from -3 to 3
Outputs:
- solution: float32 [128, 256, 1024], P('gx', 'gy', 'gz')
- residual: float32 [128, 256, 1024], P('gx', 'gy', 'gz')
- norms: float32 [4], replicated
All inputs are finite; a program needn't handle non-finite values.
Results may differ from a plain program's by a relative error of at most 0.0001.
Values sent between devices are 32-bit elements; how exact they have to be, the bound alone decides.
No kernel may reach another device: no remote copies, remote signals or barrier semaphores. Data moves between devices by JAX's collectives and lax.ppermute only.
A program may use at most 128 MiB of HBM per device.

v0:
```python
import jax
import jax.numpy as jnp
from jax import lax
from jax.sharding import Mesh
from jax.sharding import PartitionSpec as P

HALF = 4
GY = ("gy_0", "gy_1")
GX_GY_GZ = ("gx", "gy_0", "gy_1", "gz")
relaxation = 0.45


def padded_2(block, sides, width):
    for axis, dim in sides:
        count = lax.axis_size(axis)
        forward = [(i, i + 1) for i in range(count - 1)]
        backward = [(target, source) for source, target in forward]
        low = lax.ppermute(
            lax.slice_in_dim(block, block.shape[dim] - width, None, axis=dim), axis, forward
        )
        high = lax.ppermute(lax.slice_in_dim(block, 0, width, axis=dim), axis, backward)
        block = jnp.concatenate([low, block, high], axis=dim)
    return block


def padded_3(array, sides, width):
    edges = {}
    for axis, dim in sides:
        size, length = (lax.axis_size(axis), array.shape[dim])
        up = [(i, (i + 1) % size) for i in range(size - 1)]
        last = lax.slice_in_dim(array, length - width, length, axis=dim)
        first = lax.slice_in_dim(array, 0, width, axis=dim)
        edges[dim] = (
            lax.ppermute(last, axis, up),
            lax.ppermute(first, axis, [(b, a) for a, b in up]),
        )
    done = []
    for _, dim in sides:
        low, high = edges[dim]
        around = [(width, width) if d in done else (0, 0) for d in range(array.ndim)]
        array = jnp.concatenate([jnp.pad(low, around), array, jnp.pad(high, around)], axis=dim)
        done.append(dim)
    return array


def by_axis(array, axes):
    for axis in axes:
        array = lax.psum(array, axis)
    return array


def band_offsets():
    return [j - HALF for j in range(HALF)] + [j - HALF + 1 for j in range(HALF, 2 * HALF)]


def forward_band(padded, weights):
    count = weights.shape[1]
    result = padded[:, :, HALF : HALF + count]
    for j, offset in enumerate(band_offsets()):
        result = (
            result + weights[j][None, None, :] * padded[:, :, HALF + offset : HALF + offset + count]
        )
    return result


def backward_band(padded, transposed):
    count = transposed.shape[1]
    result = padded[:, :, HALF : HALF + count]
    for j, offset in enumerate(band_offsets()):
        result = (
            result
            + transposed[j][None, None, :] * padded[:, :, HALF - offset : HALF - offset + count]
        )
    return result


def transposed_weights(padded, count):
    return jnp.stack(
        [
            padded[j, HALF - offset : HALF - offset + count]
            for j, offset in enumerate(band_offsets())
        ]
    )


def combine(field, back, near, stiffness):
    return back + stiffness * (6.0 * field - near)


def diagonal_of(transposed, stiffness):
    return 1.0 + jnp.sum(transposed * transposed, axis=0) + 6.0 * stiffness


def coarsen(weights):
    return 0.5 * (weights[:, 0::2] + weights[:, 1::2])


def restrict_dim(padded, dim):
    half_count = (padded.shape[dim] - 2) // 2
    s0 = lax.slice_in_dim(padded, 0, 2 * half_count - 1, 2, dim)
    s1 = lax.slice_in_dim(padded, 1, 2 * half_count, 2, dim)
    s2 = lax.slice_in_dim(padded, 2, 2 * half_count + 1, 2, dim)
    s3 = lax.slice_in_dim(padded, 3, 2 * half_count + 2, 2, dim)
    return (s0 + 3.0 * s1 + 3.0 * s2 + s3) * 0.125


def prolong_dim(padded, dim):
    count = padded.shape[dim] - 2
    below = lax.slice_in_dim(padded, 0, count, 1, dim)
    centre = lax.slice_in_dim(padded, 1, count + 1, 1, dim)
    above = lax.slice_in_dim(padded, 2, count + 2, 1, dim)
    even = 0.75 * centre + 0.25 * below
    odd = 0.75 * centre + 0.25 * above
    joined = jnp.stack([even, odd], dim + 1)
    shape = list(centre.shape)
    shape[dim] = 2 * count
    return joined.reshape(shape)


def restrict_all(padded):
    for dim in range(3):
        padded = restrict_dim(padded, dim)
    return padded


def prolong_all(padded):
    for dim in range(3):
        padded = prolong_dim(padded, dim)
    return padded


def prepare(weights):
    padded = padded_2(weights, (("gz", 1),), HALF)
    return (transposed_weights(padded, weights.shape[1]), padded)


def transpose_apply(values, transposed):
    padded = padded_2(values, (("gz", 2),), HALF)
    return backward_band(padded, transposed)


def operate(field, wide_weights, transposed, stiffness):
    shape = field.shape
    column = padded_2(field, (("gz", 2),), 2 * HALF)
    side = padded_3(field, (("gx", 0), (GY, 1)), 1)
    near = side[2:, 1:-1, :] + side[:-2, 1:-1, :] + side[1:-1, 2:, :] + side[1:-1, :-2, :]
    near = (
        near
        + column[:, :, 2 * HALF + 1 : 2 * HALF + 1 + shape[2]]
        + column[:, :, 2 * HALF - 1 : 2 * HALF - 1 + shape[2]]
    )
    back = backward_band(forward_band(column, wide_weights), transposed)
    return combine(field, back, near, stiffness)


def narrow(defect):
    return restrict_all(padded_2(defect, (("gx", 0), (GY, 1), ("gz", 2)), 1))


def spread(coarse):
    return prolong_all(padded_2(coarse, (("gx", 0), (GY, 1), ("gz", 2)), 1))


def sweep(error, right, apply_fn, diag):
    return error + relaxation * (right - apply_fn(error)) / diag


def local_apply(wide_weights, transposed, stiffness):

    def apply_fn(field):
        return operate(field, wide_weights, transposed, stiffness)

    return apply_fn


def square_total(defect):
    partial_total = jnp.sum(defect * defect)
    return partial_total


def body(data, weights):
    devices = lax.axis_size("gx") * lax.axis_size(GY) * lax.axis_size("gz")
    level_weights = [weights]
    for level in range(3):
        level_weights.append(coarsen(level_weights[-1]))
    level_trans = []
    level_wide = []
    for level in range(3):
        transposed, wide = prepare(level_weights[level])
        level_trans.append(transposed)
        level_wide.append(wide)
    rhs = transpose_apply(data, level_trans[0])
    right = rhs
    rights, errors, diags, totals, counts = ([], [], [], [], [])
    for level in range(3):
        stiffness = 0.25**level
        diag = diagonal_of(level_trans[level], stiffness)
        apply_fn = local_apply(level_wide[level], level_trans[level], stiffness)
        error = relaxation * right / diag
        error = sweep(error, right, apply_fn, diag)
        defect = right - apply_fn(error)
        totals.append(square_total(defect))
        counts.append(defect.size * devices)
        rights.append(right)
        errors.append(error)
        diags.append(diag)
        right = narrow(defect)
    stiffness = 0.25**3
    coarse_trans, coarse_wide = prepare(level_weights[3])
    diag = diagonal_of(coarse_trans, stiffness)
    apply_fn = local_apply(coarse_wide, coarse_trans, stiffness)
    coarse = relaxation * right / diag
    coarse = sweep(coarse, right, apply_fn, diag)
    correction = spread(coarse)
    for level in (2, 1, 0):
        apply_fn = local_apply(level_wide[level], level_trans[level], 0.25**level)
        update = errors[level] + correction
        update = sweep(update, rights[level], apply_fn, diags[level])
        update = sweep(update, rights[level], apply_fn, diags[level])
        if level > 0:
            correction = spread(update)
        coarse = update
    residual = rhs - operate(coarse, level_wide[0], level_trans[0], 1.0)
    totals.append(square_total(residual))
    counts.append(residual.size * devices)
    totals = list(jax.tree.map(lambda part: by_axis(part, GX_GY_GZ), tuple(totals)))
    norms = jnp.sqrt(jnp.stack([totals[k] / counts[k] for k in range(4)]))
    return (coarse, residual, norms)


def solution(mesh):
    split = Mesh(
        mesh.devices.reshape(mesh.shape["gx"], 4, 2, mesh.shape["gz"]), ("gx", "gy_0", "gy_1", "gz")
    )
    placed = (P("gx", GY, "gz"), P(None, "gz"))
    return jax.shard_map(
        body,
        mesh=split,
        in_specs=placed,
        out_specs=(P("gx", GY, "gz"), P("gx", GY, "gz"), P()),
        check_vma=False,
    )
```

profile of v0, /device:TPU:32, one launch (start us, length us, event | category | flops | bytes accessed | tf_op | source)
XLA Modules:
  0.0 798.7 jit_solution(13713375748327662424)
XLA Ops:
  21.1 4.9 collective-permute-start.23
  72.2 8.8 %multiply_divide_fusion = (f32[32,32,128]{1,0,2:T(8,128)S(1)}, f32[32,32,128]{1,0,2:T(8,128)}) fusion(f32[128]{0:T(128)S(1)} %broadcast_add_fusion.3, f32[32,32,128]{1,0,2:T(8,128)} %copy.613, f32[128]{0:T(128)S(1)} %bitcast.214, f32[32,32,128]{1,0,2:T(8,128)} %copy.612, f32[128]{0:T(128)S(1)} %bitcast.220, f32[32,32,128]{1,0,2:T(8,128)} %copy.611, ...), kind=kLoop, calls=%fused_computation.310 | loop fusion | flops 2359296 | bytes 5771776 | tf_op jit(solution)/shard_map/div | solution.py:199
  114.4 12.2 %fusion.92 = f32[32,32,128]{1,0,2:T(8,128)S(1)} fusion(f32[32,32,128]{1,0,2:T(8,128)} %copy-done.4, f32[32,32,128]{1,0,2:T(8,128)S(1)} %copy-done.5, f32[32,32,8]{1,0,2:T(8,128)S(1)} %collective-permute-done.5, f32[32,32,8]{1,0,2:T(8,128)S(1)} %collective-permute-done.4, f32[32,1,128]{1,0,2:T(8,128)S(1)} %copy-done.17, ...), kind=kLoop, calls=%fused_computation.158 | loop fusion | flops 5767168 | bytes 6427136 | tf_op jit(solution)/shard_map/add | solution.py:165
  161.2 5.9 multiply_reduce_fusion.1
  188.3 5.4 collective-permute-start.20
  195.8 4.9 collective-permute-done.21
  204.1 6.3 slice.2087
  210.4 6.3 slice.2088
  216.7 6.4 slice.2089
  223.1 6.4 slice.2090
  231.9 6.4 slice.2091
  238.4 6.6 slice.2092
  244.9 6.6 slice.2093
  251.5 6.6 slice.2094
  294.9 4.9 collective-permute-start.33
  368.6 5.1 collective-permute-start.50
  458.6 5.3 collective-permute-start.74
  654.5 5.4 fusion.75
  662.7 5.1 collective-permute-start.118
  695.9 12.2 %fusion.65 = f32[32,32,128]{1,0,2:T(8,128)S(1)} fusion(f32[32,32,128]{1,0,2:T(8,128)} %copy-done, f32[32,32,128]{1,0,2:T(8,128)S(1)} %copy-done.8, f32[32,32,8]{1,0,2:T(8,128)S(1)} %collective-permute-done.119, f32[32,32,8]{1,0,2:T(8,128)S(1)} %collective-permute-done.118, f32[32,1,128]{1,0,2:T(8,128)S(1)} %copy-done.19, ...), kind=kLoop, calls=%fused_computation.131 | loop fusion | flops 5767168 | bytes 6427136 | tf_op jit(solution)/shard_map/add | solution.py:165
  744.0 6.7 multiply_reduce_fusion
  750.8 10.1 %all-reduce.30 = (f32[]{:T(128)}, f32[]{:T(128)}, f32[]{:T(128)}, f32[]{:T(128)}) all-reduce(f32[]{:T(128)} %get-tuple-element.37, f32[]{:T(128)} %get-tuple-element.35, f32[]{:T(128)} %get-tuple-element.33, f32[]{:T(128)} %get-tuple-element.31), channel_id=1, replica_groups=mesh['gx'=4,'gy_0'=4,'gy_1'=2,'gz'=8] {'gx'}, use_global_device_ids=true, to_apply=%region_20.21 | all-reduce | flops 4 | bytes 32 | tf_op jit(solution)/shard_map/psum | solution.py:48
  760.8 10.0 %all-reduce.29 = (f32[]{:T(128)}, f32[]{:T(128)}, f32[]{:T(128)}, f32[]{:T(128)}) all-reduce(f32[]{:T(128)} %get-tuple-element.23, f32[]{:T(128)} %get-tuple-element.24, f32[]{:T(128)} %get-tuple-element.25, f32[]{:T(128)} %get-tuple-element.26), channel_id=1, replica_groups=mesh['gx'=4,'gy_0'=4,'gy_1'=2,'gz'=8] {'gy_0'}, use_global_device_ids=true, to_apply=%region_21.22 | all-reduce | flops 4 | bytes 32 | tf_op jit(solution)/shard_map/psum | solution.py:48
  774.0 17.8 %all-reduce.28 = (f32[]{:T(128)}, f32[]{:T(128)}, f32[]{:T(128)}, f32[]{:T(128)}) all-reduce(f32[]{:T(128)} %get-tuple-element.27, f32[]{:T(128)} %get-tuple-element.28, f32[]{:T(128)} %get-tuple-element.29, f32[]{:T(128)} %get-tuple-element.30), channel_id=1, replica_groups=mesh['gx'=4,'gy_0'=4,'gy_1'=2,'gz'=8] {'gz'}, use_global_device_ids=true, to_apply=%region_23.24 | all-reduce | flops 4 | bytes 32 | tf_op jit(solution)/shard_map/psum | solution.py:48
  (762 shorter events, 614.8 us)
Async XLA Ops:
  1.5 19.6 %collective-permute-start = (f32[8,4]{1,0:T(8,128)S(1)}, f32[8,4]{1,0:T(8,128)S(1)}, u32[]{:S(2)}, u32[]{:S(2)}) collective-permute-start(f32[8,4]{1,0:T(8,128)S(1)} %get-tuple-element.305), channel_id=1, source_target_pairs={{1,0},{2,1},{3,2},{4,3},{5,4},{6,5},{7,6},{9,8},{10,9},{11,10},{12... | collective-permute-start | bytes 392 | tf_op jit(solution)/shard_map/ppermute | solution.py:21
  5.3 20.8 %collective-permute-start.2 = (f32[8,4]{1,0:T(8,128)S(1)}, f32[8,4]{1,0:T(8,128)S(1)}, u32[]{:S(2)}, u32[]{:S(2)}) collective-permute-start(f32[8,4]{1,0:T(8,128)S(1)} %get-tuple-element.304), channel_id=1, source_target_pairs={{0,1},{1,2},{2,3},{3,4},{4,5},{5,6},{6,7},{8,9},{9,10},{10,11},{11... | collective-permute-start | bytes 392 | tf_op jit(solution)/shard_map/ppermute | solution.py:18
  9.5 34.2 %collective-permute-start.3 = (f32[32,32,4]{2,1,0:T(8,128)S(1)}, f32[32,32,4]{2,1,0:T(8,128)S(1)}, u32[]{:S(2)}, u32[]{:S(2)}) collective-permute-start(f32[32,32,4]{2,1,0:T(8,128)S(1)} %get-tuple-element.122), channel_id=1, source_target_pairs={{0,1},{1,2},{2,3},{3,4},{4,5},{5,6},{6,7},{8,9},{9,10},{10,11},{11... | collective-permute-start | bytes 49160 | tf_op jit(solution)/shard_map/ppermute | solution.py:18
  13.4 31.4 %collective-permute-start.1 = (f32[32,32,4]{2,1,0:T(8,128)}, f32[32,32,4]{2,1,0:T(8,128)}, u32[]{:S(2)}, u32[]{:S(2)}) collective-permute-start(f32[32,32,4]{2,1,0:T(8,128)} %get-tuple-element.121), channel_id=1, source_target_pairs={{1,0},{2,1},{3,2},{4,3},{5,4},{6,5},{7,6},{9,8},{10,9},{11,10},{12... | collective-permute-start | bytes 49160 | tf_op jit(solution)/shard_map/ppermute | solution.py:21
  15.8 14.3 %collective-permute-start.22 = (f32[8,4]{1,0:T(8,128)S(1)}, f32[8,4]{1,0:T(8,128)S(1)}, u32[]{:S(2)}, u32[]{:S(2)}) collective-permute-start(f32[8,4]{1,0:T(8,128)S(1)} %get-tuple-element.303), channel_id=1, source_target_pairs={{1,0},{2,1},{3,2},{4,3},{5,4},{6,5},{7,6},{9,8},{10,9},{11,10},{12... | collective-permute-start | bytes 392 | tf_op jit(solution)/shard_map/ppermute | solution.py:21
  83.7 27.5 %collective-permute-start.4 = (f32[32,32,8]{1,0,2:T(8,128)S(1)}, f32[32,32,8]{1,0,2:T(8,128)S(1)}, u32[]{:S(2)}, u32[]{:S(2)}) collective-permute-start(f32[32,32,8]{1,0,2:T(8,128)S(1)} %get-tuple-element.79), channel_id=1, source_target_pairs={{0,1},{1,2},{2,3},{3,4},{4,5},{5,6},{6,7},{8,9},{9,10},{10,11},{11... | collective-permute-start | bytes 98312 | tf_op jit(solution)/shard_map/ppermute | solution.py:18
  87.9 23.3 %collective-permute-start.5 = (f32[32,32,8]{1,0,2:T(8,128)S(1)}, f32[32,32,8]{1,0,2:T(8,128)S(1)}, u32[]{:S(2)}, u32[]{:S(2)}) collective-permute-start(f32[32,32,8]{1,0,2:T(8,128)S(1)} %get-tuple-element.80), channel_id=1, source_target_pairs={{1,0},{2,1},{3,2},{4,3},{5,4},{6,5},{7,6},{9,8},{10,9},{11,10},{12... | collective-permute-start | bytes 98312 | tf_op jit(solution)/shard_map/ppermute | solution.py:21
  99.6 14.3 %collective-permute-start.6 = (f32[1,32,128]{1,0,2:T(1,128)S(1)}, f32[1,32,128]{1,0,2:T(1,128)S(1)}, u32[]{:S(2)}, u32[]{:S(2)}) collective-permute-start(f32[1,32,128]{1,0,2:T(1,128)S(1)} %get-tuple-element.78), channel_id=1, source_target_pairs={{64,0},{128,64},{192,128},{65,1},{129,65},{193,129},{66,2},{130,66... | collective-permute-start | bytes 49160 | tf_op jit(solution)/shard_map/ppermute | solution.py:35
  129.4 28.6 %collective-permute-start.10 = (f32[32,32,8]{1,0,2:T(8,128)S(1)}, f32[32,32,8]{1,0,2:T(8,128)S(1)}, u32[]{:S(2)}, u32[]{:S(2)}) collective-permute-start(f32[32,32,8]{1,0,2:T(8,128)S(1)} %get-tuple-element.74), channel_id=1, source_target_pairs={{0,1},{1,2},{2,3},{3,4},{4,5},{5,6},{6,7},{8,9},{9,10},{10,11},{11... | collective-permute-start | bytes 98312 | tf_op jit(solution)/shard_map/ppermute | solution.py:18
  134.2 23.8 %collective-permute-start.11 = (f32[32,32,8]{1,0,2:T(8,128)S(1)}, f32[32,32,8]{1,0,2:T(8,128)S(1)}, u32[]{:S(2)}, u32[]{:S(2)}) collective-permute-start(f32[32,32,8]{1,0,2:T(8,128)S(1)} %get-tuple-element.73), channel_id=1, source_target_pairs={{1,0},{2,1},{3,2},{4,3},{5,4},{6,5},{7,6},{9,8},{10,9},{11,10},{12... | collective-permute-start | bytes 98312 | tf_op jit(solution)/shard_map/ppermute | solution.py:21
  145.9 14.8 %collective-permute-start.12 = (f32[1,32,128]{1,0,2:T(1,128)S(1)}, f32[1,32,128]{1,0,2:T(1,128)S(1)}, u32[]{:S(2)}, u32[]{:S(2)}) collective-permute-start(f32[1,32,128]{1,0,2:T(1,128)S(1)} %get-tuple-element.72), channel_id=1, source_target_pairs={{64,0},{128,64},{192,128},{65,1},{129,65},{193,129},{66,2},{130,66... | collective-permute-start | bytes 49160 | tf_op jit(solution)/shard_map/ppermute | solution.py:35
  368.6 14.1 %collective-permute-start.50 = (f32[8,8,8]{1,0,2:T(8,128)S(1)}, f32[8,8,8]{1,0,2:T(8,128)S(1)}, u32[]{:S(2)}, u32[]{:S(2)}) collective-permute-start(f32[8,8,8]{1,0,2:T(8,128)S(1)} %get-tuple-element.163), channel_id=1, source_target_pairs={{0,1},{1,2},{2,3},{3,4},{4,5},{5,6},{6,7},{8,9},{9,10},{10,11},{11... | collective-permute-start | bytes 6152 | tf_op jit(solution)/shard_map/ppermute | solution.py:18
  373.7 13.5 %collective-permute-start.51 = (f32[8,8,8]{1,0,2:T(8,128)S(1)}, f32[8,8,8]{1,0,2:T(8,128)S(1)}, u32[]{:S(2)}, u32[]{:S(2)}) collective-permute-start(f32[8,8,8]{1,0,2:T(8,128)S(1)} %get-tuple-element.162), channel_id=1, source_target_pairs={{1,0},{2,1},{3,2},{4,3},{5,4},{6,5},{7,6},{9,8},{10,9},{11,10},{12... | collective-permute-start | bytes 6152 | tf_op jit(solution)/shard_map/ppermute | solution.py:21
  560.7 13.6 %collective-permute-start.100 = (f32[16,16,8]{1,0,2:T(8,128)S(1)}, f32[16,16,8]{1,0,2:T(8,128)S(1)}, u32[]{:S(2)}, u32[]{:S(2)}) collective-permute-start(f32[16,16,8]{1,0,2:T(8,128)S(1)} %get-tuple-element.99), channel_id=1, source_target_pairs={{0,1},{1,2},{2,3},{3,4},{4,5},{5,6},{6,7},{8,9},{9,10},{10,11},{11... | collective-permute-start | bytes 24584 | tf_op jit(solution)/shard_map/ppermute | solution.py:18
  621.5 28.8 %collective-permute-start.112 = (f32[32,32,8]{1,0,2:T(8,128)S(1)}, f32[32,32,8]{1,0,2:T(8,128)S(1)}, u32[]{:S(2)}, u32[]{:S(2)}) collective-permute-start(f32[32,32,8]{1,0,2:T(8,128)S(1)} %get-tuple-element.65), channel_id=1, source_target_pairs={{0,1},{1,2},{2,3},{3,4},{4,5},{5,6},{6,7},{8,9},{9,10},{10,11},{11... | collective-permute-start | bytes 98312 | tf_op jit(solution)/shard_map/ppermute | solution.py:18
  625.8 24.4 %collective-permute-start.113 = (f32[32,32,8]{1,0,2:T(8,128)S(1)}, f32[32,32,8]{1,0,2:T(8,128)S(1)}, u32[]{:S(2)}, u32[]{:S(2)}) collective-permute-start(f32[32,32,8]{1,0,2:T(8,128)S(1)} %get-tuple-element.66), channel_id=1, source_target_pairs={{1,0},{2,1},{3,2},{4,3},{5,4},{6,5},{7,6},{9,8},{10,9},{11,10},{12... | collective-permute-start | bytes 98312 | tf_op jit(solution)/shard_map/ppermute | solution.py:21
  638.6 14.8 %collective-permute-start.114 = (f32[1,32,128]{1,0,2:T(1,128)S(1)}, f32[1,32,128]{1,0,2:T(1,128)S(1)}, u32[]{:S(2)}, u32[]{:S(2)}) collective-permute-start(f32[1,32,128]{1,0,2:T(1,128)S(1)} %get-tuple-element.64), channel_id=1, source_target_pairs={{64,0},{128,64},{192,128},{65,1},{129,65},{193,129},{66,2},{130,66... | collective-permute-start | bytes 49160 | tf_op jit(solution)/shard_map/ppermute | solution.py:35
  662.7 30.1 %collective-permute-start.118 = (f32[32,32,8]{1,0,2:T(8,128)S(1)}, f32[32,32,8]{1,0,2:T(8,128)S(1)}, u32[]{:S(2)}, u32[]{:S(2)}) collective-permute-start(f32[32,32,8]{1,0,2:T(8,128)S(1)} %get-tuple-element.59), channel_id=1, source_target_pairs={{0,1},{1,2},{2,3},{3,4},{4,5},{5,6},{6,7},{8,9},{9,10},{10,11},{11... | collective-permute-start | bytes 98312 | tf_op jit(solution)/shard_map/ppermute | solution.py:18
  667.9 24.9 %collective-permute-start.119 = (f32[32,32,8]{1,0,2:T(8,128)S(1)}, f32[32,32,8]{1,0,2:T(8,128)S(1)}, u32[]{:S(2)}, u32[]{:S(2)}) collective-permute-start(f32[32,32,8]{1,0,2:T(8,128)S(1)} %get-tuple-element.60), channel_id=1, source_target_pairs={{1,0},{2,1},{3,2},{4,3},{5,4},{6,5},{7,6},{9,8},{10,9},{11,10},{12... | collective-permute-start | bytes 98312 | tf_op jit(solution)/shard_map/ppermute | solution.py:21
  681.0 14.5 %collective-permute-start.120 = (f32[1,32,128]{1,0,2:T(1,128)S(1)}, f32[1,32,128]{1,0,2:T(1,128)S(1)}, u32[]{:S(2)}, u32[]{:S(2)}) collective-permute-start(f32[1,32,128]{1,0,2:T(1,128)S(1)} %get-tuple-element.58), channel_id=1, source_target_pairs={{64,0},{128,64},{192,128},{65,1},{129,65},{193,129},{66,2},{130,66... | collective-permute-start | bytes 49160 | tf_op jit(solution)/shard_map/ppermute | solution.py:35
  711.0 29.9 %collective-permute-start.124 = (f32[32,32,8]{1,0,2:T(8,128)S(1)}, f32[32,32,8]{1,0,2:T(8,128)S(1)}, u32[]{:S(2)}, u32[]{:S(2)}) collective-permute-start(f32[32,32,8]{1,0,2:T(8,128)S(1)} %get-tuple-element.54), channel_id=1, source_target_pairs={{0,1},{1,2},{2,3},{3,4},{4,5},{5,6},{6,7},{8,9},{9,10},{10,11},{11... | collective-permute-start | bytes 98312 | tf_op jit(solution)/shard_map/ppermute | solution.py:18
  714.9 26.0 %collective-permute-start.125 = (f32[32,32,8]{1,0,2:T(8,128)S(1)}, f32[32,32,8]{1,0,2:T(8,128)S(1)}, u32[]{:S(2)}, u32[]{:S(2)}) collective-permute-start(f32[32,32,8]{1,0,2:T(8,128)S(1)} %get-tuple-element.53), channel_id=1, source_target_pairs={{1,0},{2,1},{3,2},{4,3},{5,4},{6,5},{7,6},{9,8},{10,9},{11,10},{12... | collective-permute-start | bytes 98312 | tf_op jit(solution)/shard_map/ppermute | solution.py:21
  723.4 14.6 %collective-permute-start.129 = (f32[32,1,128]{2,0,1:T(8,128)S(1)}, f32[32,1,128]{2,0,1:T(8,128)S(1)}, u32[]{:S(2)}, u32[]{:S(2)}) collective-permute-start(f32[32,1,128]{2,0,1:T(8,128)S(1)} %copy.599), channel_id=1, source_target_pairs={{0,8},{8,16},{16,24},{24,32},{32,40},{40,48},{48,56},{1,9},{9,17},... | collective-permute-start | bytes 49160 | tf_op jit(solution)/shard_map/ppermute | solution.py:34
  729.0 14.6 %collective-permute-start.126 = (f32[1,32,128]{1,0,2:T(1,128)S(1)}, f32[1,32,128]{1,0,2:T(1,128)S(1)}, u32[]{:S(2)}, u32[]{:S(2)}) collective-permute-start(f32[1,32,128]{1,0,2:T(1,128)S(1)} %get-tuple-element.52), channel_id=1, source_target_pairs={{64,0},{128,64},{192,128},{65,1},{129,65},{193,129},{66,2},{130,66... | collective-permute-start | bytes 49160 | tf_op jit(solution)/shard_map/ppermute | solution.py:35
  (230 other events, 6268.7 us)
where the time goes:
time: 807 us; the launch traced here: 799 us
  starting transfers between devices  360 us (45%)
  local copies, waits for them, and re-layouts  202 us (25%)
  other arithmetic  108 us (13%)
  waiting for transfers between devices  79.2 us (10%)
  blocking collectives  41 us (5%)
    ppermute x37, starting transfers between devices, padded_2(): lax.ppermute(lax.slice_in_dim(block, block.shape[dim] - width, None, axis...  143 us
    ppermute x28, starting transfers between devices, padded_3(): lax.ppermute(last, axis, up)  114 us
    ppermute x37, waiting for transfers between devices, padded_2(): lax.ppermute(lax.slice_in_dim(block, 0, width, axis=dim), axis, backward)  69.1 us
    ppermute x37, starting transfers between devices, padded_2(): lax.ppermute(lax.slice_in_dim(block, 0, width, axis=dim), axis, backward)  66.4 us
    unnamed x264, local copies, waits for them, and re-layouts  42.3 us
    psum x4, blocking collectives, by_axis(): array = lax.psum(array, axis)  41 us
    add x10, other arithmetic, sweep(): return error + relaxation * (right - apply_fn(error)) / diag  38.5 us
    ppermute x28, starting transfers between devices, padded_3(): lax.ppermute(first, axis, [(b, a) for a, b in up])  36.5 us
  transfers between devices with their start and end apart: 130, of which 33 were waited for; matrix products, arithmetic and copies ran while one was open for 13% of the time, Pallas kernels for 0%

commit v1 on v0

--- a/solution.py
+++ b/solution.py
@@ -45,7 +45,7 @@
 
 def by_axis(array, axes):
     for axis in axes:
-        array = lax.psum(array, axis)
+        array = jnp.sum(lax.all_gather(array, axis), axis=0)
     return array
 
 

time: 807 us -> 835 us (1.035)
  local copies, waits for them, and re-layouts: 202 us -> 227 us
  other arithmetic: 108 us -> 119 us
    psum x4 -> x0, blocking collectives: 41 us -> none  [by_axis(): array = lax.psum(array, axis)]
    unnamed x0 -> x4, blocking collectives: none -> 38.2 us
    unnamed x264 -> x314, local copies, waits for them, and re-layouts: 42.3 us -> 66.1 us
    reduce_sum x0 -> x16, other arithmetic: none -> 9.61 us  [by_axis(): array = jnp.sum(lax.all_gather(array, axis), axis=0)]
  transfers between devices with their start and end apart: 130 -> 130, of which waited for: 33 -> 32; matrix products, arithmetic and copies ran while one was open for 13% -> 13% of each run, Pallas kernels for 0% -> 0%
where the time goes in v1:
time: 835 us; the launch traced here: 826 us
  starting transfers between devices  360 us (43%)
  local copies, waits for them, and re-layouts  227 us (27%)
  other arithmetic  119 us (14%)
  waiting for transfers between devices  74.4 us (9%)
  blocking collectives  38.2 us (5%)
    ppermute x37, starting transfers between devices, padded_2(): lax.ppermute(lax.slice_in_dim(block, block.shape[dim] - width, None, axis...  143 us
    ppermute x28, starting transfers between devices, padded_3(): lax.ppermute(last, axis, up)  114 us
    ppermute x37, waiting for transfers between devices, padded_2(): lax.ppermute(lax.slice_in_dim(block, 0, width, axis=dim), axis, backward)  67.1 us
    ppermute x37, starting transfers between devices, padded_2(): lax.ppermute(lax.slice_in_dim(block, 0, width, axis=dim), axis, backward)  66.8 us
    unnamed x314, local copies, waits for them, and re-layouts  66.1 us
    unnamed x4, blocking collectives  38.2 us
    add x10, other arithmetic, sweep(): return error + relaxation * (right - apply_fn(error)) / diag  37.2 us
    ppermute x28, starting transfers between devices, padded_3(): lax.ppermute(first, axis, [(b, a) for a, b in up])  36.5 us
  transfers between devices with their start and end apart: 130, of which 32 were waited for; matrix products, arithmetic and copies ran while one was open for 13% of the time, Pallas kernels for 0%

profile of v1, /device:TPU:32, one launch (start us, length us, event | category | flops | bytes accessed | tf_op | source)
XLA Modules:
  0.0 826.3 jit_solution(14758932335222680890)
XLA Ops:
  74.1 8.8 %multiply_divide_fusion = (f32[32,32,128]{1,0,2:T(8,128)S(1)}, f32[32,32,128]{1,0,2:T(8,128)}) fusion(f32[128]{0:T(128)S(1)} %broadcast_add_fusion.3, f32[32,32,128]{1,0,2:T(8,128)} %copy.613, f32[128]{0:T(128)S(1)} %bitcast.234, f32[32,32,128]{1,0,2:T(8,128)} %copy.612, f32[128]{0:T(128)S(1)} %bitcast.240, f32[32,32,128]{1,0,2:T(8,128)} %copy.611, ...), kind=kLoop, calls=%fused_computation.310 | loop fusion | flops 2359296 | bytes 5771776 | tf_op jit(solution)/shard_map/div | solution.py:199
  116.4 11.6 %fusion.92 = f32[32,32,128]{1,0,2:T(8,128)S(1)} fusion(f32[32,32,128]{1,0,2:T(8,128)} %copy-done.4, f32[32,32,128]{1,0,2:T(8,128)S(1)} %copy-done.5, f32[32,32,8]{1,0,2:T(8,128)S(1)} %collective-permute-done.5, f32[32,32,8]{1,0,2:T(8,128)S(1)} %collective-permute-done.4, f32[32,1,128]{1,0,2:T(8,128)S(1)} %copy-done.17, ...), kind=kLoop, calls=%fused_computation.158 | loop fusion | flops 5767168 | bytes 6427136 | tf_op jit(solution)/shard_map/add | solution.py:165
  162.4 5.9 multiply_reduce_fusion.1
  189.6 5.4 collective-permute-start.20
  197.0 4.9 collective-permute-done.21
  205.3 6.3 slice.2087
  211.6 6.3 slice.2088
  217.9 6.4 slice.2089
  224.3 6.4 slice.2090
  233.2 6.4 slice.2091
  239.6 6.6 slice.2092
  246.2 6.6 slice.2093
  252.8 6.5 slice.2094
  262.2 4.9 collective-permute-start.24
  296.2 4.9 collective-permute-start.33
  369.8 5.1 collective-permute-start.50
  459.8 5.3 collective-permute-start.74
  655.9 5.4 fusion.75
  664.1 5.1 collective-permute-start.118
  697.4 11.6 %fusion.65 = f32[32,32,128]{1,0,2:T(8,128)S(1)} fusion(f32[32,32,128]{1,0,2:T(8,128)} %copy-done, f32[32,32,128]{1,0,2:T(8,128)S(1)} %copy-done.8, f32[32,32,8]{1,0,2:T(8,128)S(1)} %collective-permute-done.119, f32[32,32,8]{1,0,2:T(8,128)S(1)} %collective-permute-done.118, f32[32,1,128]{1,0,2:T(8,128)S(1)} %copy-done.19, ...), kind=kLoop, calls=%fused_computation.131 | loop fusion | flops 5767168 | bytes 6427136 | tf_op jit(solution)/shard_map/add | solution.py:165
  742.5 6.7 multiply_reduce_fusion
  751.5 9.4 %all-reduce.46 = (f32[4]{0:T(128)S(1)}, f32[4]{0:T(128)S(1)}, f32[4]{0:T(128)S(1)}, f32[4]{0:T(128)S(1)}) all-reduce(f32[4]{0:T(128)S(1)} %dynamic-update-slice.12, f32[4]{0:T(128)S(1)} %dynamic-update-slice.8, f32[4]{0:T(128)S(1)} %dynamic-update-slice.4, f32[4]{0:T(128)S(1)} %dynamic-update-slice), channel_id=1, replica_groups=mesh['gx'=4,'gy_0'=4,'gy_1'=2,'gz'=8] {'gx'}, use_global_device_ids=true, to_apply=%add.40 | all-reduce | flops 16 | bytes 128
  769.4 9.3 %all-reduce.45 = (f32[4]{0:T(128)S(1)}, f32[4]{0:T(128)S(1)}, f32[4]{0:T(128)S(1)}, f32[4]{0:T(128)S(1)}) all-reduce(f32[4]{0:T(128)S(1)} %dynamic-update-slice.13, f32[4]{0:T(128)S(1)} %dynamic-update-slice.9, f32[4]{0:T(128)S(1)} %dynamic-update-slice.5, ...), channel_id=1, replica_groups=mesh['gx'=4,'gy_0'=4,'gy_1'=2,'gz'=8] {'gy_0'}, use_global_device_ids=true, to_apply=%add.41 | all-reduce | flops 16 | bytes 128
  799.9 17.1 %all-reduce.44 = (f32[8]{0:T(128)S(1)}, f32[8]{0:T(128)S(1)}, f32[8]{0:T(128)S(1)}, f32[8]{0:T(128)S(1)}) all-reduce(f32[8]{0:T(128)S(1)} %dynamic-update-slice.15, f32[8]{0:T(128)S(1)} %dynamic-update-slice.11, f32[8]{0:T(128)S(1)} %dynamic-update-slice.7, ...), channel_id=1, replica_groups=mesh['gx'=4,'gy_0'=4,'gy_1'=2,'gz'=8] {'gz'}, use_global_device_ids=true, to_apply=%add.43 | all-reduce | flops 32 | bytes 256
  (828 shorter events, 645.7 us)
Async XLA Ops:
  1.5 20.3 %collective-permute-start = (f32[8,4]{1,0:T(8,128)S(1)}, f32[8,4]{1,0:T(8,128)S(1)}, u32[]{:S(2)}, u32[]{:S(2)}) collective-permute-start(f32[8,4]{1,0:T(8,128)S(1)} %get-tuple-element.305), channel_id=1, source_target_pairs={{1,0},{2,1},{3,2},{4,3},{5,4},{6,5},{7,6},{9,8},{10,9},{11,10},{12... | collective-permute-start | bytes 392 | tf_op jit(solution)/shard_map/ppermute | solution.py:21
  5.3 20.7 %collective-permute-start.2 = (f32[8,4]{1,0:T(8,128)S(1)}, f32[8,4]{1,0:T(8,128)S(1)}, u32[]{:S(2)}, u32[]{:S(2)}) collective-permute-start(f32[8,4]{1,0:T(8,128)S(1)} %get-tuple-element.304), channel_id=1, source_target_pairs={{0,1},{1,2},{2,3},{3,4},{4,5},{5,6},{6,7},{8,9},{9,10},{10,11},{11... | collective-permute-start | bytes 392 | tf_op jit(solution)/shard_map/ppermute | solution.py:18
  9.5 34.2 %collective-permute-start.3 = (f32[32,32,4]{2,1,0:T(8,128)S(1)}, f32[32,32,4]{2,1,0:T(8,128)}, u32[]{:S(2)}, u32[]{:S(2)}) collective-permute-start(f32[32,32,4]{2,1,0:T(8,128)S(1)} %get-tuple-element.122), channel_id=1, source_target_pairs={{0,1},{1,2},{2,3},{3,4},{4,5},{5,6},{6,7},{8,9},{9,10},{10,11},{11... | collective-permute-start | bytes 49160 | tf_op jit(solution)/shard_map/ppermute | solution.py:18
  13.4 34.2 %collective-permute-start.1 = (f32[32,32,4]{2,1,0:T(8,128)}, f32[32,32,4]{2,1,0:T(8,128)}, u32[]{:S(2)}, u32[]{:S(2)}) collective-permute-start(f32[32,32,4]{2,1,0:T(8,128)} %get-tuple-element.121), channel_id=1, source_target_pairs={{1,0},{2,1},{3,2},{4,3},{5,4},{6,5},{7,6},{9,8},{10,9},{11,10},{12... | collective-permute-start | bytes 49160 | tf_op jit(solution)/shard_map/ppermute | solution.py:21
  85.7 27.5 %collective-permute-start.4 = (f32[32,32,8]{1,0,2:T(8,128)S(1)}, f32[32,32,8]{1,0,2:T(8,128)S(1)}, u32[]{:S(2)}, u32[]{:S(2)}) collective-permute-start(f32[32,32,8]{1,0,2:T(8,128)S(1)} %get-tuple-element.79), channel_id=1, source_target_pairs={{0,1},{1,2},{2,3},{3,4},{4,5},{5,6},{6,7},{8,9},{9,10},{10,11},{11... | collective-permute-start | bytes 98312 | tf_op jit(solution)/shard_map/ppermute | solution.py:18
  89.9 23.4 %collective-permute-start.5 = (f32[32,32,8]{1,0,2:T(8,128)S(1)}, f32[32,32,8]{1,0,2:T(8,128)S(1)}, u32[]{:S(2)}, u32[]{:S(2)}) collective-permute-start(f32[32,32,8]{1,0,2:T(8,128)S(1)} %get-tuple-element.80), channel_id=1, source_target_pairs={{1,0},{2,1},{3,2},{4,3},{5,4},{6,5},{7,6},{9,8},{10,9},{11,10},{12... | collective-permute-start | bytes 98312 | tf_op jit(solution)/shard_map/ppermute | solution.py:21
  101.5 14.4 %collective-permute-start.6 = (f32[1,32,128]{1,0,2:T(1,128)S(1)}, f32[1,32,128]{1,0,2:T(1,128)S(1)}, u32[]{:S(2)}, u32[]{:S(2)}) collective-permute-start(f32[1,32,128]{1,0,2:T(1,128)S(1)} %get-tuple-element.78), channel_id=1, source_target_pairs={{64,0},{128,64},{192,128},{65,1},{129,65},{193,129},{66,2},{130,66... | collective-permute-start | bytes 49160 | tf_op jit(solution)/shard_map/ppermute | solution.py:35
  130.7 28.5 %collective-permute-start.10 = (f32[32,32,8]{1,0,2:T(8,128)S(1)}, f32[32,32,8]{1,0,2:T(8,128)S(1)}, u32[]{:S(2)}, u32[]{:S(2)}) collective-permute-start(f32[32,32,8]{1,0,2:T(8,128)S(1)} %get-tuple-element.74), channel_id=1, source_target_pairs={{0,1},{1,2},{2,3},{3,4},{4,5},{5,6},{6,7},{8,9},{9,10},{10,11},{11... | collective-permute-start | bytes 98312 | tf_op jit(solution)/shard_map/ppermute | solution.py:18
  135.6 23.7 %collective-permute-start.11 = (f32[32,32,8]{1,0,2:T(8,128)S(1)}, f32[32,32,8]{1,0,2:T(8,128)S(1)}, u32[]{:S(2)}, u32[]{:S(2)}) collective-permute-start(f32[32,32,8]{1,0,2:T(8,128)S(1)} %get-tuple-element.73), channel_id=1, source_target_pairs={{1,0},{2,1},{3,2},{4,3},{5,4},{6,5},{7,6},{9,8},{10,9},{11,10},{12... | collective-permute-start | bytes 98312 | tf_op jit(solution)/shard_map/ppermute | solution.py:21
  147.2 14.8 %collective-permute-start.12 = (f32[1,32,128]{1,0,2:T(1,128)S(1)}, f32[1,32,128]{1,0,2:T(1,128)S(1)}, u32[]{:S(2)}, u32[]{:S(2)}) collective-permute-start(f32[1,32,128]{1,0,2:T(1,128)S(1)} %get-tuple-element.72), channel_id=1, source_target_pairs={{64,0},{128,64},{192,128},{65,1},{129,65},{193,129},{66,2},{130,66... | collective-permute-start | bytes 49160 | tf_op jit(solution)/shard_map/ppermute | solution.py:35
  369.8 14.1 %collective-permute-start.50 = (f32[8,8,8]{1,0,2:T(8,128)S(1)}, f32[8,8,8]{1,0,2:T(8,128)S(1)}, u32[]{:S(2)}, u32[]{:S(2)}) collective-permute-start(f32[8,8,8]{1,0,2:T(8,128)S(1)} %get-tuple-element.163), channel_id=1, source_target_pairs={{0,1},{1,2},{2,3},{3,4},{4,5},{5,6},{6,7},{8,9},{9,10},{10,11},{11... | collective-permute-start | bytes 6152 | tf_op jit(solution)/shard_map/ppermute | solution.py:18
  375.0 13.5 %collective-permute-start.51 = (f32[8,8,8]{1,0,2:T(8,128)S(1)}, f32[8,8,8]{1,0,2:T(8,128)S(1)}, u32[]{:S(2)}, u32[]{:S(2)}) collective-permute-start(f32[8,8,8]{1,0,2:T(8,128)S(1)} %get-tuple-element.162), channel_id=1, source_target_pairs={{1,0},{2,1},{3,2},{4,3},{5,4},{6,5},{7,6},{9,8},{10,9},{11,10},{12... | collective-permute-start | bytes 6152 | tf_op jit(solution)/shard_map/ppermute | solution.py:21
  562.0 13.6 %collective-permute-start.100 = (f32[16,16,8]{1,0,2:T(8,128)S(1)}, f32[16,16,8]{1,0,2:T(8,128)S(1)}, u32[]{:S(2)}, u32[]{:S(2)}) collective-permute-start(f32[16,16,8]{1,0,2:T(8,128)S(1)} %get-tuple-element.99), channel_id=1, source_target_pairs={{0,1},{1,2},{2,3},{3,4},{4,5},{5,6},{6,7},{8,9},{9,10},{10,11},{11... | collective-permute-start | bytes 24584 | tf_op jit(solution)/shard_map/ppermute | solution.py:18
  622.8 28.8 %collective-permute-start.112 = (f32[32,32,8]{1,0,2:T(8,128)S(1)}, f32[32,32,8]{1,0,2:T(8,128)S(1)}, u32[]{:S(2)}, u32[]{:S(2)}) collective-permute-start(f32[32,32,8]{1,0,2:T(8,128)S(1)} %get-tuple-element.65), channel_id=1, source_target_pairs={{0,1},{1,2},{2,3},{3,4},{4,5},{5,6},{6,7},{8,9},{9,10},{10,11},{11... | collective-permute-start | bytes 98312 | tf_op jit(solution)/shard_map/ppermute | solution.py:18
  627.6 24.1 %collective-permute-start.113 = (f32[32,32,8]{1,0,2:T(8,128)S(1)}, f32[32,32,8]{1,0,2:T(8,128)S(1)}, u32[]{:S(2)}, u32[]{:S(2)}) collective-permute-start(f32[32,32,8]{1,0,2:T(8,128)S(1)} %get-tuple-element.66), channel_id=1, source_target_pairs={{1,0},{2,1},{3,2},{4,3},{5,4},{6,5},{7,6},{9,8},{10,9},{11,10},{12... | collective-permute-start | bytes 98312 | tf_op jit(solution)/shard_map/ppermute | solution.py:21
  639.9 14.9 %collective-permute-start.114 = (f32[1,32,128]{1,0,2:T(1,128)S(1)}, f32[1,32,128]{1,0,2:T(1,128)S(1)}, u32[]{:S(2)}, u32[]{:S(2)}) collective-permute-start(f32[1,32,128]{1,0,2:T(1,128)S(1)} %get-tuple-element.64), channel_id=1, source_target_pairs={{64,0},{128,64},{192,128},{65,1},{129,65},{193,129},{66,2},{130,66... | collective-permute-start | bytes 49160 | tf_op jit(solution)/shard_map/ppermute | solution.py:35
  641.2 13.6 %collective-permute-start.115 = (f32[1,32,128]{1,0,2:T(1,128)S(1)}, f32[1,32,128]{1,0,2:T(1,128)S(1)}, u32[]{:S(2)}, u32[]{:S(2)}) collective-permute-start(f32[1,32,128]{1,0,2:T(1,128)S(1)} %get-tuple-element.63), channel_id=1, source_target_pairs={{0,64},{64,128},{128,192},{1,65},{65,129},{129,193},{2,66},{66,130... | collective-permute-start | bytes 49160 | tf_op jit(solution)/shard_map/ppermute | solution.py:34
  664.1 30.1 %collective-permute-start.118 = (f32[32,32,8]{1,0,2:T(8,128)S(1)}, f32[32,32,8]{1,0,2:T(8,128)S(1)}, u32[]{:S(2)}, u32[]{:S(2)}) collective-permute-start(f32[32,32,8]{1,0,2:T(8,128)S(1)} %get-tuple-element.59), channel_id=1, source_target_pairs={{0,1},{1,2},{2,3},{3,4},{4,5},{5,6},{6,7},{8,9},{9,10},{10,11},{11... | collective-permute-start | bytes 98312 | tf_op jit(solution)/shard_map/ppermute | solution.py:18
  669.3 25.0 %collective-permute-start.119 = (f32[32,32,8]{1,0,2:T(8,128)S(1)}, f32[32,32,8]{1,0,2:T(8,128)S(1)}, u32[]{:S(2)}, u32[]{:S(2)}) collective-permute-start(f32[32,32,8]{1,0,2:T(8,128)S(1)} %get-tuple-element.60), channel_id=1, source_target_pairs={{1,0},{2,1},{3,2},{4,3},{5,4},{6,5},{7,6},{9,8},{10,9},{11,10},{12... | collective-permute-start | bytes 98312 | tf_op jit(solution)/shard_map/ppermute | solution.py:21
  677.8 13.6 %collective-permute-start.123 = (f32[32,1,128]{2,0,1:T(8,128)S(1)}, f32[32,1,128]{2,0,1:T(8,128)S(1)}, u32[]{:S(2)}, u32[]{:S(2)}) collective-permute-start(f32[32,1,128]{2,0,1:T(8,128)S(1)} %copy.595), channel_id=1, source_target_pairs={{0,8},{8,16},{16,24},{24,32},{32,40},{40,48},{48,56},{1,9},{9,17},... | collective-permute-start | bytes 49160 | tf_op jit(solution)/shard_map/ppermute | solution.py:34
  682.4 14.6 %collective-permute-start.120 = (f32[1,32,128]{1,0,2:T(1,128)S(1)}, f32[1,32,128]{1,0,2:T(1,128)S(1)}, u32[]{:S(2)}, u32[]{:S(2)}) collective-permute-start(f32[1,32,128]{1,0,2:T(1,128)S(1)} %get-tuple-element.58), channel_id=1, source_target_pairs={{64,0},{128,64},{192,128},{65,1},{129,65},{193,129},{66,2},{130,66... | collective-permute-start | bytes 49160 | tf_op jit(solution)/shard_map/ppermute | solution.py:35
  711.8 27.6 %collective-permute-start.124 = (f32[32,32,8]{1,0,2:T(8,128)S(1)}, f32[32,32,8]{1,0,2:T(8,128)S(1)}, u32[]{:S(2)}, u32[]{:S(2)}) collective-permute-start(f32[32,32,8]{1,0,2:T(8,128)S(1)} %get-tuple-element.54), channel_id=1, source_target_pairs={{0,1},{1,2},{2,3},{3,4},{4,5},{5,6},{6,7},{8,9},{9,10},{10,11},{11... | collective-permute-start | bytes 98312 | tf_op jit(solution)/shard_map/ppermute | solution.py:18
  715.7 23.7 %collective-permute-start.125 = (f32[32,32,8]{1,0,2:T(8,128)S(1)}, f32[32,32,8]{1,0,2:T(8,128)S(1)}, u32[]{:S(2)}, u32[]{:S(2)}) collective-permute-start(f32[32,32,8]{1,0,2:T(8,128)S(1)} %get-tuple-element.53), channel_id=1, source_target_pairs={{1,0},{2,1},{3,2},{4,3},{5,4},{6,5},{7,6},{9,8},{10,9},{11,10},{12... | collective-permute-start | bytes 98312 | tf_op jit(solution)/shard_map/ppermute | solution.py:21
  727.8 14.4 %collective-permute-start.126 = (f32[1,32,128]{1,0,2:T(1,128)S(1)}, f32[1,32,128]{1,0,2:T(1,128)S(1)}, u32[]{:S(2)}, u32[]{:S(2)}) collective-permute-start(f32[1,32,128]{1,0,2:T(1,128)S(1)} %get-tuple-element.52), channel_id=1, source_target_pairs={{64,0},{128,64},{192,128},{65,1},{129,65},{193,129},{66,2},{130,66... | collective-permute-start | bytes 49160 | tf_op jit(solution)/shard_map/ppermute | solution.py:35
  (237 other events, 6420.0 us)
